TPU v7x, 256 devices: a whole 4x4x8 slice. The times are simulated.
256 devices in a mesh: dp: 32 (over x_hi, z, core), mp: 8 (over x_lo, y).
Axes of the slice: x: 4 (x_hi: 2, x_lo: 2; x = x_hi * 2 + x_lo), y: 4, z: 8, core: 2. Of those that a mesh axis runs over, the one named last changes fastest.
Arguments:
- context: bfloat16 [8192, 6144], P('dp', 'mp'), may hold values from -6 to 6
- out_grad: bfloat16 [8192, 6144], P('dp', 'mp'), may hold values from -1.0546875 to 1.0546875
- master: float32 [8, 36864, 128], P('mp', 'dp'), may hold values from -0.078125 to 0.078125
- moment_one: float32 [8, 36864, 128], P('mp', 'dp'), may hold values from -3 to 3
- moment_two: float32 [8, 36864, 128], P('mp', 'dp'), may hold values from 1 to 64
- new_owner: int32 [32], replicated, may hold values from 0 to 31, as said below
- old_pieces: int32 [32, 32, 36], replicated, may hold values from 0 to 36863, as said below
Outputs:
- proj_out: bfloat16 [8192, 6144], P('dp', 'mp')
- master_out: float32 [8, 36864, 128], P('mp', 'dp')
- moment_one_out: float32 [8, 36864, 128], P('mp', 'dp')
- moment_two_out: float32 [8, 36864, 128], P('mp', 'dp')
Inputs may be any that keep to these rules, and one draw needn't show every extreme that they name: `new_owner`: each index of dp appears exactly once. Every block number appears exactly once; old_pieces[i, j, :] lie from new_owner[j] * 1152 to new_owner[j] * 1152 + 1151.
All inputs are finite; a program needn't handle non-finite values.
Results may differ from a plain program's by a relative error of at most 0.015.
Values may be sent and summed in bfloat16 or wider, within the bound.
No kernel may reach another device: no remote copies, remote signals or barrier semaphores. Data moves between devices by JAX's collectives and lax.ppermute only.
A program may use at most 64 MiB of HBM per device.

v0:
```python
import jax
import jax.numpy as jnp
from jax import lax
from jax.sharding import Mesh, PartitionSpec as P

beta_one = 0.9
beta_two = 0.999
learn_rate = 0.001
decay_rate = 0.1
epsilon = 1e-08
step_count = 100.0
DP = ("xh", "z", "c")
MP = ("xl", "y")
DL = ("xh", "c")


def adamw(weights, first_moment, second_moment, gradient):
    first_new = beta_one * first_moment + (1.0 - beta_one) * gradient
    second_new = beta_two * second_moment + (1.0 - beta_two) * gradient * gradient
    corrected_first = first_new / (1.0 - beta_one**step_count)
    corrected_second = second_new / (1.0 - beta_two**step_count)
    update = corrected_first / (jnp.sqrt(corrected_second) + epsilon)
    weights_new = weights - learn_rate * (update + decay_rate * weights)
    return (weights_new, first_new, second_new)


def one_hot(index, count):
    rows = lax.broadcasted_iota(jnp.int32, (count, index.shape[0]), 0)
    return (rows == index[None, :]).astype(jnp.bfloat16)


def local(context, out_grad, master, moment_one, moment_two, new_owner, old_pieces):
    f32, bf16 = (jnp.float32, jnp.bfloat16)
    n_dp, n_mp = (lax.axis_size(DP), lax.axis_size(MP))
    n_z, n_dl = (lax.axis_size("z"), lax.axis_size(DL))
    n_xh, n_c = (lax.axis_size("xh"), lax.axis_size("c"))
    d = lax.axis_index(DP)
    blocks, width = master.shape[1:]
    tokens, cols = context.shape
    per_dev = cols // width
    per_row = per_dev * n_mp
    rows = blocks // per_row
    own_slab = new_owner[d]
    positions = (
        lax.dynamic_index_in_dim(old_pieces, d, 1, keepdims=False) - own_slab * blocks
    ).reshape(-1)
    w_in = lax.all_to_all(master[0].astype(bf16), DP, 0, 0, tiled=True)
    moments = jnp.concatenate([moment_one[0], moment_two[0]], axis=1).astype(bf16)
    m_in = lax.all_to_all(moments, DP, 0, 0, tiled=True)
    owner_order = new_owner.reshape(n_xh, n_z, n_c).transpose(0, 2, 1).reshape(-1)
    wanted = (owner_order[:, None] * rows + jnp.arange(rows, dtype=jnp.int32)[None]).reshape(-1)
    columns = lax.broadcasted_iota(jnp.int32, (cols, cols), 1)
    select = (columns == wanted[:, None]).astype(bf16)
    ct = lax.dot_general(
        select, context, (((1,), (1,)), ((), ())), preferred_element_type=f32
    ).astype(bf16)
    ct = lax.all_to_all(ct.reshape(n_dl, n_z * rows, tokens), DL, 0, 0, tiled=True)
    ct = lax.all_gather(ct, MP, axis=0, tiled=False)
    ct = (
        ct.reshape(n_mp, n_dl, n_z, rows, tokens)
        .transpose(0, 2, 3, 1, 4)
        .reshape(n_mp * n_z * rows, n_dl * tokens)
    )
    og = lax.all_gather(out_grad, DL, axis=0, tiled=True)
    grad = jnp.dot(ct, og, preferred_element_type=f32).astype(bf16)
    grad = lax.psum_scatter(
        grad.reshape(n_mp, n_z, rows, cols), "z", scatter_dimension=1, tiled=True
    )
    grad = lax.all_to_all(grad.reshape(n_mp, rows, cols), MP, 0, 0, tiled=True)
    grad = (
        grad.reshape(n_mp, rows, per_dev, width)
        .transpose(1, 0, 2, 3)
        .reshape(blocks, width)
        .astype(f32)
    )
    w_at = positions % per_row * rows + positions // per_row
    w_t = jnp.dot(one_hot(w_at, blocks), w_in, preferred_element_type=f32).astype(bf16)
    w_t = lax.all_to_all(w_t.reshape(n_mp, per_dev, rows, width), MP, 0, 0, tiled=True)
    w_t = lax.all_gather(w_t, "z", axis=0, tiled=False)
    w_t = w_t.transpose(1, 0, 3, 2, 4).reshape(n_mp * n_z * rows, cols)
    out = lax.dot_general(ct, w_t, (((0,), (0,)), ((), ())), preferred_element_type=f32).astype(
        bf16
    )
    proj_out = lax.psum_scatter(out, DL, scatter_dimension=0, tiled=True)
    placed = jnp.dot(
        one_hot(positions, blocks),
        jnp.concatenate([w_in, m_in], axis=1),
        preferred_element_type=f32,
    )
    weights, first_moment, second_moment = (
        placed[:, i * width : (i + 1) * width] for i in range(3)
    )
    weights_new, first_new, second_new = adamw(weights, first_moment, second_moment, grad)
    return (proj_out, weights_new[None], first_new[None], second_new[None])


def solution(mesh):
    fine = Mesh(mesh.devices.reshape(2, 8, 2, 2, 4), DP[:2] + ("c",) + MP)
    placed = (P(DP, MP), P(DP, MP), P(MP, DP, None), P(MP, DP, None), P(MP, DP, None), P(), P())
    return jax.shard_map(
        local,
        mesh=fine,
        in_specs=placed,
        out_specs=(P(DP, MP), P(MP, DP, None), P(MP, DP, None), P(MP, DP, None)),
        check_vma=False,
    )
```

profile of v0, /device:TPU:1, one launch (start us, length us, event | category | flops | bytes accessed | tf_op | source)
XLA Modules:
  0.0 251.5 jit_solution(14708763887175539069)
XLA Ops:
  7.2 0.0 copy-start
  7.2 0.0 copy-start.1
  7.2 0.0 all-gather.8.cloned.1.call-start
  7.2 0.7 broadcast_multiply_fusion
  8.0 0.1 mul.71
  8.1 0.1 copy.21
  8.1 0.1 mul.73
  8.2 0.1 iota_add_fusion
  8.3 0.1 add.75
  8.4 0.0 copy-done
  8.4 0.0 copy-start.5
  8.4 0.6 fusion.12
  9.0 14.1 %all_to_all.33 = bf16[4,192,256]{2,1,0:T(8,128)(2,1)} all-to-all(bf16[4,192,256]{2,1,0:T(8,128)(2,1)S(1)} %bitcast.42), channel_id=1, replica_groups=mesh['xh'=2,'z'=8,'c'=2,'xl'=2,'y'=4] {'xh','c'}, dimensions={0} | all-to-all | bytes 786432 | tf_op jit(solution)/shard_map/all_to_all | solution.py:57
  23.2 0.0 all-gather.8.cloned.1.call-update
  23.2 0.0 all-gather.6.cloned.1.call-start
  23.2 0.7 all-gather.6.cloned.1.call-update
  23.9 0.0 copy-done.1
  24.0 0.8 convert_element_type.38
  24.8 9.1 %all-to-all-start.1 = ((bf16[32,36,128]{2,1,0:T(8,128)(2,1)}), bf16[32,36,128]{2,1,0:T(8,128)(2,1)S(1)}, u32[]{:S(2)}, u32[]{:S(2)}) async-start(bf16[32,36,128]{2,1,0:T(8,128)(2,1)} %convert_element_type.38), calls=%async_computation.1 | async-start | bytes 655360 | tf_op jit(solution)/shard_map/all_to_all | solution.py:47
  33.8 0.0 all-gather.10.cloned.1.call-start
  33.9 0.0 copy-done.5
  33.9 0.6 dynamic_slice.8
  35.2 1.0 subtract_reduce_fusion
  36.1 0.1 sub.28
  36.3 12.1 %all-to-all-done.1 = bf16[32,36,128]{2,1,0:T(8,128)(2,1)S(1)} async-done(((bf16[32,36,128]{2,1,0:T(8,128)(2,1)}), bf16[32,36,128]{2,1,0:T(8,128)(2,1)S(1)}, u32[]{:S(2)}, u32[]{:S(2)}) %all-to-all-start.1) | async-done | bytes 294944 | tf_op jit(solution)/shard_map/all_to_all | solution.py:47
  48.4 0.1 all_to_all.23
  48.4 0.0 copy-start.3
  48.4 1.0 fusion.4
  49.5 16.6 %all_to_all.34 = bf16[8,6,24,128]{3,2,1,0:T(8,128)(2,1)} all-to-all(bf16[8,6,24,128]{3,2,1,0:T(8,128)(2,1)S(1)} %bitcast.44), channel_id=1, replica_groups=mesh['xh'=2,'z'=8,'c'=2,'xl'=2,'y'=4] {'xl','y'}, dimensions={0} | all-to-all | bytes 589824 | tf_op jit(solution)/shard_map/all_to_all | solution.py:78
  66.0 0.0 all-gather.10.cloned.1.call-update
  66.0 0.0 reduce-scatter.5.cloned.1.call-start
  66.1 8.6 %all-gather.8.cloned.1.call-done = bf16[32,192,256]{2,1,0:T(8,128)(2,1)} async-done(((bf16[4,192,256]{2,1,0:T(8,128)(2,1)}), bf16[32,192,256]{2,1,0:T(8,128)(2,1)}) %all-gather.8.cloned.1.call-update) | async-done | bytes 3145744 | tf_op jit(solution)/shard_map/all_gather | solution.py:58
  74.7 5.9 %copy.22 = bf16[8,8,24,4,256]{4,3,2,1,0:T(4,128)(2,1)S(1)} copy(bf16[8,8,24,4,256]{4,2,1,3,0:T(8,128)(2,1)} %bitcast.35) | data formatting | bytes 6291456 | tf_op jit(solution)/shard_map/transpose | solution.py:61
  80.6 0.0 copy-done.3
  80.6 0.8 copy.26
  81.4 22.4 %all-gather.6.cloned.1.call-done = bf16[1024,768]{1,0:T(8,128)(2,1)} async-done(((bf16[256,768]{1,0:T(8,128)(2,1)}), bf16[1024,768]{1,0:T(8,128)(2,1)}) %all-gather.6.cloned.1.call-update) | async-done | bytes 1572880 | tf_op jit(solution)/shard_map/all_gather | solution.py:64
  103.7 4.2 %convolution_convert_fusion = bf16[1536,768]{1,0:T(8,128)(2,1)S(1)} fusion(bf16[1536,1024]{1,0:T(8,128)(2,1)S(1)} %bitcast.36, bf16[1024,768]{1,0:T(8,128)(2,1)} %all-gather.6.cloned.1.call-done), kind=kOutput, calls=%fused_computation.4 | convolution fusion | flops 2417098752 | bytes 7077888 | tf_op jit(solution)/shard_map/dot_general | solution.py:65
  107.9 1.6 copy.24
  109.6 0.0 reduce-scatter.5.cloned.1.call-update
  109.6 0.0 reduce-scatter.3.cloned.1.call-start
  109.6 32.6 %all-gather.10.cloned.1.call-done = bf16[64,6,24,128]{3,2,1,0:T(8,128)(2,1)} async-done(((bf16[8,6,24,128]{3,2,1,0:T(8,128)(2,1)}), bf16[64,6,24,128]{3,2,1,0:T(8,128)(2,1)}) %all-gather.10.cloned.1.call-update) | async-done | bytes 2359312 | tf_op jit(solution)/shard_map/all_gather | solution.py:79
  142.2 2.5 %copy.23 = bf16[8,8,24,6,128]{4,3,2,1,0:T(8,128)(2,1)S(1)} copy(bf16[8,8,24,6,128]{4,2,3,0,1:T(8,128)(2,1)} %bitcast.41) | data formatting | bytes 4718592 | tf_op jit(solution)/shard_map/transpose | solution.py:80
  144.7 3.9 %fusion.9 = bf16[1024,768]{1,0:T(8,128)(2,1)} fusion(bf16[1536,1024]{1,0:T(8,128)(2,1)S(1)} %bitcast.37, bf16[192,8,6,128]{3,2,1,0:T(8,128)(2,1)S(1)} %bitcast.39), kind=kOutput, calls=%fused_computation.13 | convolution fusion | flops 2416705536 | bytes 7077888 | tf_op jit(solution)/shard_map/dot_general | solution.py:81
  148.6 0.0 copy-start.2
  148.6 0.0 reduce-scatter.3.cloned.1.call-update
  148.6 1.2 convert.12
  149.8 0.1 concatenate.13
  149.9 0.0 copy-done.2
  149.9 0.1 concatenate.12
  150.0 0.0 copy-start.4
  150.0 0.1 pad_maximum_fusion
  150.1 39.4 %all_to_all.35 = bf16[32,36,256]{2,1,0:T(8,128)(2,1)S(1)} all-to-all(bf16[32,36,256]{2,1,0:T(8,128)(2,1)S(1)} %pad_maximum_fusion), channel_id=1, replica_groups=mesh['xh'=2,'z'=8,'c'=2,'xl'=2,'y'=4] {'xh','z','c'}, dimensions={0} | all-to-all | bytes 1179648 | tf_op jit(solution)/shard_map/all_to_all | solution.py:49
  189.4 0.1 all_to_all.26
  189.6 9.6 %reduce-scatter.5.cloned.1.call-done = bf16[8,1,24,768]{3,2,0,1:T(8,128)(2,1)} async-done(((bf16[8,8,24,768]{3,2,0,1:T(8,128)(2,1)}), bf16[8,1,24,768]{3,2,0,1:T(8,128)(2,1)}) %reduce-scatter.5.cloned.1.call-update) | async-done | bytes 294928 | tf_op jit(solution)/shard_map/reduce_scatter | solution.py:66
  199.2 4.8 %all-to-all-start.4 = ((bf16[8,24,768]{2,1,0:T(8,128)(2,1)}), bf16[8,24,768]{2,1,0:T(8,128)(2,1)S(1)}, u32[]{:S(2)}, u32[]{:S(2)}) async-start(bf16[8,24,768]{2,1,0:T(8,128)(2,1)} %bitcast.43), calls=%async_computation.6 | async-start | bytes 589824 | tf_op jit(solution)/shard_map/all_to_all | solution.py:69
  204.0 0.0 copy-done.4
  204.0 2.8 %fusion.1 = f32[1152,384]{1,0:T(8,128)} fusion(s32[1152]{0:T(1024)S(1)} %sub.28, bf16[1152,256]{1,0:T(8,128)(2,1)S(1)} %all_to_all.26, bf16[1152,128]{1,0:T(8,128)(2,1)S(1)} %copy-done.4), kind=kOutput, calls=%fused_computation.3 | convolution fusion | flops 1022312448 | bytes 2658816 | tf_op jit(solution)/shard_map/dot_general | solution.py:85
  206.8 3.4 %all-to-all-done.4 = bf16[8,24,768]{2,1,0:T(8,128)(2,1)S(1)} async-done(((bf16[8,24,768]{2,1,0:T(8,128)(2,1)}), bf16[8,24,768]{2,1,0:T(8,128)(2,1)S(1)}, u32[]{:S(2)}, u32[]{:S(2)}) %all-to-all-start.4) | async-done | bytes 294944 | tf_op jit(solution)/shard_map/all_to_all | solution.py:69
  210.2 0.3 reshape.109
  210.5 0.1 copy.25
  210.6 0.1 reshape.108
  210.7 2.9 %fusion.20 = (f32[1,1152,128]{2,1,0:T(8,128)}, f32[1,1152,128]{2,1,0:T(8,128)}, f32[1,1152,128]{2,1,0:T(8,128)}) fusion(f32[1152,128]{1,0:T(8,128)S(1)} %reshape.108, f32[1152,384]{1,0:T(8,128)} %fusion.1), kind=kLoop, calls=%fused_computation.27 | loop fusion | flops 2211840 | bytes 4128768 | tf_op jit(solution)/shard_map/broadcast_in_dim | solution.py:94
  213.6 31.3 %reduce-scatter.3.cloned.1.call-done = bf16[256,768]{1,0:T(8,128)(2,1)} async-done(((bf16[1024,768]{1,0:T(8,128)(2,1)}), bf16[256,768]{1,0:T(8,128)(2,1)}) %reduce-scatter.3.cloned.1.call-update) | async-done | bytes 393232 | tf_op jit(solution)/shard_map/reduce_scatter | solution.py:84
  (3 shorter events, 0.1 us)
Async XLA Ops:
  7.2 1.2 copy-start
  7.2 16.8 %copy-start.1 = (f32[1,1152,128]{2,1,0:T(8,128)S(1)}, f32[1,1152,128]{2,1,0:T(8,128)}, u32[]{:S(2)}) copy-start(f32[1,1152,128]{2,1,0:T(8,128)} %param.9) | copy-start | bytes 1769476
  7.2 67.5 %all-gather.8.cloned.1.call-start = ((), (), s32[]{:S(2)}) async-start(), calls=%async_computation.10 | async-start | bytes 3538944 | tf_op jit(solution)/shard_map/all_gather | solution.py:58
  8.4 25.5 %copy-start.5 = (s32[32]{0:T(128)S(1)}, s32[32]{0:T(128)}, u32[]{:S(2)}) copy-start(s32[32]{0:T(128)} %param.12) | copy-start | bytes 388
  23.2 80.6 %all-gather.6.cloned.1.call-start = ((), (), s32[]{:S(2)}) async-start(), calls=%async_computation.8 | async-start | bytes 1966080 | tf_op jit(solution)/shard_map/all_gather | solution.py:64
  24.8 23.6 %all-to-all-start.1 = ((bf16[32,36,128]{2,1,0:T(8,128)(2,1)}), bf16[32,36,128]{2,1,0:T(8,128)(2,1)S(1)}, u32[]{:S(2)}, u32[]{:S(2)}) async-start(bf16[32,36,128]{2,1,0:T(8,128)(2,1)} %convert_element_type.38), calls=%async_computation.1 | async-start | bytes 655360 | tf_op jit(solution)/shard_map/all_to_all | solution.py:47
  33.8 108.4 %all-gather.10.cloned.1.call-start = ((), (), s32[]{:S(2)}) async-start(), calls=%async_computation.11 | async-start | bytes 2654208 | tf_op jit(solution)/shard_map/all_gather | solution.py:79
  48.4 32.2 %copy-start.3 = (bf16[1152,128]{1,0:T(8,128)(2,1)}, bf16[1152,128]{1,0:T(8,128)(2,1)S(1)}, u32[]{:S(2)}) copy-start(bf16[1152,128]{1,0:T(8,128)(2,1)S(1)} %all_to_all.23) | copy-start | bytes 884740
  66.0 133.2 %reduce-scatter.5.cloned.1.call-start = ((), (), s32[]{:S(2)}) async-start(), calls=%async_computation.9 | async-start | bytes 2654208 | tf_op jit(solution)/shard_map/reduce_scatter | solution.py:66
  109.6 135.3 %reduce-scatter.3.cloned.1.call-start = ((), (), s32[]{:S(2)}) async-start(), calls=%async_computation.7 | async-start | bytes 1966080 | tf_op jit(solution)/shard_map/reduce_scatter | solution.py:84
  148.6 1.2 copy-start.2
  150.0 54.0 %copy-start.4 = (bf16[1152,128]{1,0:T(8,128)(2,1)S(1)}, bf16[1152,128]{1,0:T(8,128)(2,1)}, u32[]{:S(2)}) copy-start(bf16[1152,128]{1,0:T(8,128)(2,1)} %copy-done.3) | copy-start | bytes 884740
  199.2 11.0 %all-to-all-start.4 = ((bf16[8,24,768]{2,1,0:T(8,128)(2,1)}), bf16[8,24,768]{2,1,0:T(8,128)(2,1)S(1)}, u32[]{:S(2)}, u32[]{:S(2)}) async-start(bf16[8,24,768]{2,1,0:T(8,128)(2,1)} %bitcast.43), calls=%async_computation.6 | async-start | bytes 589824 | tf_op jit(solution)/shard_map/all_to_all | solution.py:69
Sparse Core Ops, SparseCore 0:
  23.3 51.3 all-gather.7
  76.5 27.2 all-gather.5
  105.5 36.6 all-gather.9
  144.6 54.5 reduce-scatter.4
  202.4 42.4 reduce-scatter.2
where the time goes:
time: 252 us; the launch traced here: 251 us
  waiting for transfers between devices  121 us (48%)
  blocking collectives  70.1 us (28%)
  between operations  14.7 us (6%)
  starting transfers between devices  14 us (6%)
  local copies, waits for them, and re-layouts  13.5 us (5%)
  matrix products  12.5 us (5%)
  other arithmetic  6.02 us (2%)
    all_to_all x1, blocking collectives, local(): m_in = lax.all_to_all(moments, DP, 0, 0, tiled=True)  39.4 us
    all_gather x1, waiting for transfers between devices, local(): w_t = lax.all_gather(w_t, 'z', axis=0, tiled=False)  32.6 us
    reduce_scatter x1, waiting for transfers between devices, local(): proj_out = lax.psum_scatter(out, DL, scatter_dimension=0, tiled=True)  31.3 us
    all_gather x1, waiting for transfers between devices, local(): og = lax.all_gather(out_grad, DL, axis=0, tiled=True)  22.4 us
    all_to_all x1, blocking collectives, local(): lax.all_to_all(w_t.reshape(n_mp, per_dev, rows, width), MP, 0, 0, tiled=T...  16.6 us
    all_to_all x1, blocking collectives, local(): lax.all_to_all(ct.reshape(n_dl, n_z * rows, tokens), DL, 0, 0, tiled=True)  14.1 us
    all_to_all x1, waiting for transfers between devices, local(): w_in = lax.all_to_all(master[0].astype(bf16), DP, 0, 0, tiled=True)  12.1 us
    reduce_scatter x1, waiting for transfers between devices, local(): lax.psum_scatter(grad.reshape(n_mp, n_z, rows, cols), 'z', scatter_dimens...  9.64 us
  transfers between devices with their start and end apart: 7, of which 7 were waited for; matrix products, arithmetic and copies ran while one was open for 12% of the time, Pallas kernels for 0%

commit v1 on v0

--- a/solution.py
+++ b/solution.py
@@ -1,3 +1,4 @@
+import functools
 import jax
 import jax.numpy as jnp
 from jax import lax
@@ -12,6 +13,22 @@
 DP = ("xh", "z", "c")
 MP = ("xl", "y")
 DL = ("xh", "c")
+
+
+def unite_wires_now(slab_in, dim_at):
+    local_next = jnp.concatenate(
+        lax.all_to_all(
+            jnp.stack([slab_in] * lax.axis_size(DL), axis=0),
+            concat_axis=0,
+            axis_name=DL,
+            split_axis=0,
+        ),
+        axis=dim_at,
+    )
+    return local_next
+
+
+handle_the_field = functools.partial(unite_wires_now, dim_at=0)
 
 
 def adamw(weights, first_moment, second_moment, gradient):
@@ -61,7 +78,7 @@
         .transpose(0, 2, 3, 1, 4)
         .reshape(n_mp * n_z * rows, n_dl * tokens)
     )
-    og = lax.all_gather(out_grad, DL, axis=0, tiled=True)
+    og = handle_the_field(out_grad)
     grad = jnp.dot(ct, og, preferred_element_type=f32).astype(bf16)
     grad = lax.psum_scatter(
         grad.reshape(n_mp, n_z, rows, cols), "z", scatter_dimension=1, tiled=True

time: 252 us -> 229 us (0.909)
  waiting for transfers between devices: 121 us -> 90.7 us
  starting transfers between devices: 14 us -> 19.3 us
    all_gather x1 -> x0, waiting for transfers between devices: 22.4 us -> none  [local(): og = lax.all_gather(out_grad, DL, axis=0, tiled=True)]
    all_gather x1, waiting for transfers between devices: 32.6 us -> 19.8 us  [local(): w_t = lax.all_gather(w_t, 'z', axis=0, tiled=False)]
    all_to_all x0 -> x1, waiting for transfers between devices: none -> 11.9 us  [unite_wires_now(): lax.all_to_all(jnp.stack([slab_in] * lax.axis_size(DL), axis=0), concat_a...]
    all_gather x1, waiting for transfers between devices: 8.58 us -> 2.7 us  [local(): ct = lax.all_gather(ct, MP, axis=0, tiled=False)]
    all_to_all x0 -> x1, starting transfers between devices: none -> 5.12 us  [unite_wires_now(): lax.all_to_all(jnp.stack([slab_in] * lax.axis_size(DL), axis=0), concat_a...]
  transfers between devices with their start and end apart: 7 -> 7, of which waited for: 7 -> 7; matrix products, arithmetic and copies ran while one was open for 12% -> 14% of each run, Pallas kernels for 0% -> 0%
where the time goes in v1:
time: 229 us; the launch traced here: 228 us
  waiting for transfers between devices  90.7 us (40%)
  blocking collectives  70.1 us (31%)
  starting transfers between devices  19.3 us (8%)
  local copies, waits for them, and re-layouts  14.8 us (6%)
  between operations  14.6 us (6%)
  matrix products  12.5 us (5%)
  other arithmetic  6.04 us (3%)
    all_to_all x1, blocking collectives, local(): m_in = lax.all_to_all(moments, DP, 0, 0, tiled=True)  39.4 us
    reduce_scatter x1, waiting for transfers between devices, local(): proj_out = lax.psum_scatter(out, DL, scatter_dimension=0, tiled=True)  31.1 us
    all_gather x1, waiting for transfers between devices, local(): w_t = lax.all_gather(w_t, 'z', axis=0, tiled=False)  19.8 us
    all_to_all x1, blocking collectives, local(): lax.all_to_all(w_t.reshape(n_mp, per_dev, rows, width), MP, 0, 0, tiled=T...  16.5 us
    all_to_all x1, blocking collectives, local(): lax.all_to_all(ct.reshape(n_dl, n_z * rows, tokens), DL, 0, 0, tiled=True)  14.2 us
    all_to_all x1, waiting for transfers between devices, local(): w_in = lax.all_to_all(master[0].astype(bf16), DP, 0, 0, tiled=True)  12.1 us
    all_to_all x1, waiting for transfers between devices, unite_wires_now(): lax.all_to_all(jnp.stack([slab_in] * lax.axis_size(DL), axis=0), concat_a...  11.9 us
    reduce_scatter x1, waiting for transfers between devices, local(): lax.psum_scatter(grad.reshape(n_mp, n_z, rows, cols), 'z', scatter_dimens...  9.7 us
  transfers between devices with their start and end apart: 7, of which 7 were waited for; matrix products, arithmetic and copies ran while one was open for 14% of the time, Pallas kernels for 0%

profile of v1, /device:TPU:1, one launch (start us, length us, event | category | flops | bytes accessed | tf_op | source)
XLA Modules:
  0.0 228.1 jit_solution(5758278040559627454)
XLA Ops:
  7.2 0.0 copy-start
  7.2 0.0 copy-start.1
  7.2 0.0 all-gather.5.cloned.1.call-start
  7.2 0.7 broadcast_multiply_fusion
  8.0 0.1 mul.71
  8.1 0.1 copy.21
  8.1 0.1 mul.73
  8.2 0.1 iota_add_fusion
  8.3 0.1 add.75
  8.4 0.0 copy-done
  8.4 0.0 copy-start.6
  8.4 0.6 fusion.12
  9.0 14.2 %all_to_all.38 = bf16[4,192,256]{2,1,0:T(8,128)(2,1)} all-to-all(bf16[4,192,256]{2,1,0:T(8,128)(2,1)S(1)} %bitcast.43), channel_id=1, replica_groups=mesh['xh'=2,'z'=8,'c'=2,'xl'=2,'y'=4] {'xh','c'}, dimensions={0} | all-to-all | bytes 786432 | tf_op jit(solution)/shard_map/all_to_all | solution.py:74
  23.2 0.0 all-gather.5.cloned.1.call-update
  23.2 0.0 copy-done.1
  23.2 0.8 convert_element_type.38
  24.0 0.0 copy-start.3
  24.0 9.2 %all-to-all-start.1 = ((bf16[32,36,128]{2,1,0:T(8,128)(2,1)}), bf16[32,36,128]{2,1,0:T(8,128)(2,1)S(1)}, u32[]{:S(2)}, u32[]{:S(2)}) async-start(bf16[32,36,128]{2,1,0:T(8,128)(2,1)} %convert_element_type.38), calls=%async_computation.1 | async-start | bytes 655360 | tf_op jit(solution)/shard_map/all_to_all | solution.py:64
  33.2 0.0 all-gather.7.cloned.1.call-start
  33.3 0.0 copy-done.6
  33.3 0.6 dynamic_slice.8
  34.5 1.0 subtract_reduce_fusion
  35.5 0.1 sub.28
  35.6 12.1 %all-to-all-done.1 = bf16[32,36,128]{2,1,0:T(8,128)(2,1)S(1)} async-done(((bf16[32,36,128]{2,1,0:T(8,128)(2,1)}), bf16[32,36,128]{2,1,0:T(8,128)(2,1)S(1)}, u32[]{:S(2)}, u32[]{:S(2)}) %all-to-all-start.1) | async-done | bytes 294944 | tf_op jit(solution)/shard_map/all_to_all | solution.py:64
  47.7 0.1 all_to_all.26
  47.8 0.0 copy-start.4
  47.8 1.0 fusion.4
  48.8 16.5 %all_to_all.39 = bf16[8,6,24,128]{3,2,1,0:T(8,128)(2,1)} all-to-all(bf16[8,6,24,128]{3,2,1,0:T(8,128)(2,1)S(1)} %bitcast.45), channel_id=1, replica_groups=mesh['xh'=2,'z'=8,'c'=2,'xl'=2,'y'=4] {'xl','y'}, dimensions={0} | all-to-all | bytes 589824 | tf_op jit(solution)/shard_map/all_to_all | solution.py:95
  65.3 0.0 all-gather.7.cloned.1.call-update
  65.4 0.0 copy-done.3
  65.4 1.3 stack.2
  66.7 0.0 copy-done.4
  66.7 5.1 %all-to-all-start.4 = ((bf16[4,256,768]{2,1,0:T(8,128)(2,1)}), bf16[4,256,768]{2,1,0:T(8,128)(2,1)}, u32[]{:S(2)}, u32[]{:S(2)}) async-start(bf16[4,256,768]{2,1,0:T(8,128)(2,1)} %stack.2), calls=%async_computation.5 | async-start | bytes 3145728 | tf_op jit(solution)/shard_map/all_to_all | solution.py:20
  71.8 0.0 reduce-scatter.5.cloned.1.call-start
  71.8 2.7 %all-gather.5.cloned.1.call-done = bf16[32,192,256]{2,1,0:T(8,128)(2,1)} async-done(((bf16[4,192,256]{2,1,0:T(8,128)(2,1)}), bf16[32,192,256]{2,1,0:T(8,128)(2,1)}) %all-gather.5.cloned.1.call-update) | async-done | bytes 3145744 | tf_op jit(solution)/shard_map/all_gather | solution.py:75
  74.5 5.9 %copy.22 = bf16[8,8,24,4,256]{4,3,2,1,0:T(4,128)(2,1)S(1)} copy(bf16[8,8,24,4,256]{4,2,1,3,0:T(8,128)(2,1)} %bitcast.36) | data formatting | bytes 6291456 | tf_op jit(solution)/shard_map/transpose | solution.py:78
  80.5 0.8 copy.26
  81.3 11.9 %all-to-all-done.4 = bf16[4,256,768]{2,1,0:T(8,128)(2,1)} async-done(((bf16[4,256,768]{2,1,0:T(8,128)(2,1)}), bf16[4,256,768]{2,1,0:T(8,128)(2,1)}, u32[]{:S(2)}, u32[]{:S(2)}) %all-to-all-start.4) | async-done | bytes 1572896 | tf_op jit(solution)/shard_map/all_to_all | solution.py:20
  93.2 4.2 %convolution_convert_fusion = bf16[1536,768]{1,0:T(8,128)(2,1)S(1)} fusion(bf16[1536,1024]{1,0:T(8,128)(2,1)S(1)} %bitcast.37, bf16[1024,768]{1,0:T(8,128)(2,1)} %bitcast.8), kind=kOutput, calls=%fused_computation.4 | convolution fusion | flops 2417098752 | bytes 7077888 | tf_op jit(solution)/shard_map/dot_general | solution.py:82
  97.4 1.6 copy.24
  99.0 0.0 reduce-scatter.5.cloned.1.call-update
  99.0 0.2 reduce-scatter.3.cloned.1.call-start
  99.2 19.8 %all-gather.7.cloned.1.call-done = bf16[64,6,24,128]{3,2,1,0:T(8,128)(2,1)} async-done(((bf16[8,6,24,128]{3,2,1,0:T(8,128)(2,1)}), bf16[64,6,24,128]{3,2,1,0:T(8,128)(2,1)}) %all-gather.7.cloned.1.call-update) | async-done | bytes 2359312 | tf_op jit(solution)/shard_map/all_gather | solution.py:96
  119.0 2.5 %copy.23 = bf16[8,8,24,6,128]{4,3,2,1,0:T(8,128)(2,1)S(1)} copy(bf16[8,8,24,6,128]{4,2,3,0,1:T(8,128)(2,1)} %bitcast.42) | data formatting | bytes 4718592 | tf_op jit(solution)/shard_map/transpose | solution.py:97
  121.6 3.9 %fusion.9 = bf16[1024,768]{1,0:T(8,128)(2,1)} fusion(bf16[1536,1024]{1,0:T(8,128)(2,1)S(1)} %bitcast.38, bf16[192,8,6,128]{3,2,1,0:T(8,128)(2,1)S(1)} %bitcast.40), kind=kOutput, calls=%fused_computation.13 | convolution fusion | flops 2416705536 | bytes 7077888 | tf_op jit(solution)/shard_map/dot_general | solution.py:98
  125.4 0.0 reduce-scatter.3.cloned.1.call-update
  125.5 1.2 convert.12
  126.6 0.1 concatenate.13
  126.7 0.0 copy-done.2
  126.7 0.1 concatenate.12
  126.8 0.0 copy-start.5
  126.8 0.1 pad_maximum_fusion
  126.9 39.4 %all_to_all.40 = bf16[32,36,256]{2,1,0:T(8,128)(2,1)S(1)} all-to-all(bf16[32,36,256]{2,1,0:T(8,128)(2,1)S(1)} %pad_maximum_fusion), channel_id=1, replica_groups=mesh['xh'=2,'z'=8,'c'=2,'xl'=2,'y'=4] {'xh','z','c'}, dimensions={0} | all-to-all | bytes 1179648 | tf_op jit(solution)/shard_map/all_to_all | solution.py:66
  166.3 0.1 all_to_all.29
  166.4 9.7 %reduce-scatter.5.cloned.1.call-done = bf16[8,1,24,768]{3,2,0,1:T(8,128)(2,1)} async-done(((bf16[8,8,24,768]{3,2,0,1:T(8,128)(2,1)}), bf16[8,1,24,768]{3,2,0,1:T(8,128)(2,1)}) %reduce-scatter.5.cloned.1.call-update) | async-done | bytes 294928 | tf_op jit(solution)/shard_map/reduce_scatter | solution.py:83
  176.1 4.7 %all-to-all-start.5 = ((bf16[8,24,768]{2,1,0:T(8,128)(2,1)}), bf16[8,24,768]{2,1,0:T(8,128)(2,1)S(1)}, u32[]{:S(2)}, u32[]{:S(2)}) async-start(bf16[8,24,768]{2,1,0:T(8,128)(2,1)} %bitcast.44), calls=%async_computation.7 | async-start | bytes 589824 | tf_op jit(solution)/shard_map/all_to_all | solution.py:86
  180.8 0.0 copy-done.5
  180.8 2.8 %fusion.1 = f32[1152,384]{1,0:T(8,128)} fusion(s32[1152]{0:T(1024)S(1)} %sub.28, bf16[1152,256]{1,0:T(8,128)(2,1)S(1)} %all_to_all.29, bf16[1152,128]{1,0:T(8,128)(2,1)S(1)} %copy-done.5), kind=kOutput, calls=%fused_computation.3 | convolution fusion | flops 1022312448 | bytes 2658816 | tf_op jit(solution)/shard_map/dot_general | solution.py:102
  183.6 3.4 %all-to-all-done.5 = bf16[8,24,768]{2,1,0:T(8,128)(2,1)S(1)} async-done(((bf16[8,24,768]{2,1,0:T(8,128)(2,1)}), bf16[8,24,768]{2,1,0:T(8,128)(2,1)S(1)}, u32[]{:S(2)}, u32[]{:S(2)}) %all-to-all-start.5) | async-done | bytes 294944 | tf_op jit(solution)/shard_map/all_to_all | solution.py:86
  187.0 0.3 reshape.115
  187.3 0.1 copy.25
  187.4 0.1 reshape.114
  187.5 2.9 %fusion.20 = (f32[1,1152,128]{2,1,0:T(8,128)}, f32[1,1152,128]{2,1,0:T(8,128)}, f32[1,1152,128]{2,1,0:T(8,128)}) fusion(f32[1152,128]{1,0:T(8,128)S(1)} %reshape.114, f32[1152,384]{1,0:T(8,128)} %fusion.1), kind=kLoop, calls=%fused_computation.27 | loop fusion | flops 2211840 | bytes 4128768 | tf_op jit(solution)/shard_map/broadcast_in_dim | solution.py:111
  190.4 31.1 %reduce-scatter.3.cloned.1.call-done = bf16[256,768]{1,0:T(8,128)(2,1)} async-done(((bf16[1024,768]{1,0:T(8,128)(2,1)}), bf16[256,768]{1,0:T(8,128)(2,1)}) %reduce-scatter.3.cloned.1.call-update) | async-done | bytes 393232 | tf_op jit(solution)/shard_map/reduce_scatter | solution.py:101
  (4 shorter events, 0.1 us)
Async XLA Ops:
  7.2 1.2 copy-start
  7.2 16.0 %copy-start.1 = (f32[1,1152,128]{2,1,0:T(8,128)S(1)}, f32[1,1152,128]{2,1,0:T(8,128)}, u32[]{:S(2)}) copy-start(f32[1,1152,128]{2,1,0:T(8,128)} %param.9) | copy-start | bytes 1769476
  7.2 67.4 %all-gather.5.cloned.1.call-start = ((), (), s32[]{:S(2)}) async-start(), calls=%async_computation.10 | async-start | bytes 3538944 | tf_op jit(solution)/shard_map/all_gather | solution.py:75
  8.4 24.9 %copy-start.6 = (s32[32]{0:T(128)S(1)}, s32[32]{0:T(128)}, u32[]{:S(2)}) copy-start(s32[32]{0:T(128)} %param.12) | copy-start | bytes 388
  24.0 41.3 %copy-start.3 = (bf16[256,768]{1,0:T(8,128)(2,1)S(1)}, bf16[256,768]{1,0:T(8,128)(2,1)}, u32[]{:S(2)}) copy-start(bf16[256,768]{1,0:T(8,128)(2,1)} %param.8) | copy-start | bytes 1179652
  24.0 23.7 %all-to-all-start.1 = ((bf16[32,36,128]{2,1,0:T(8,128)(2,1)}), bf16[32,36,128]{2,1,0:T(8,128)(2,1)S(1)}, u32[]{:S(2)}, u32[]{:S(2)}) async-start(bf16[32,36,128]{2,1,0:T(8,128)(2,1)} %convert_element_type.38), calls=%async_computation.1 | async-start | bytes 655360 | tf_op jit(solution)/shard_map/all_to_all | solution.py:64
  33.2 85.8 %all-gather.7.cloned.1.call-start = ((), (), s32[]{:S(2)}) async-start(), calls=%async_computation.11 | async-start | bytes 2654208 | tf_op jit(solution)/shard_map/all_gather | solution.py:96
  47.8 18.9 %copy-start.4 = (bf16[1152,128]{1,0:T(8,128)(2,1)}, bf16[1152,128]{1,0:T(8,128)(2,1)S(1)}, u32[]{:S(2)}) copy-start(bf16[1152,128]{1,0:T(8,128)(2,1)S(1)} %all_to_all.26) | copy-start | bytes 884740
  66.7 26.5 %all-to-all-start.4 = ((bf16[4,256,768]{2,1,0:T(8,128)(2,1)}), bf16[4,256,768]{2,1,0:T(8,128)(2,1)}, u32[]{:S(2)}, u32[]{:S(2)}) async-start(bf16[4,256,768]{2,1,0:T(8,128)(2,1)} %stack.2), calls=%async_computation.5 | async-start | bytes 3145728 | tf_op jit(solution)/shard_map/all_to_all | solution.py:20
  71.8 104.3 %reduce-scatter.5.cloned.1.call-start = ((), (), s32[]{:S(2)}) async-start(), calls=%async_computation.9 | async-start | bytes 2654208 | tf_op jit(solution)/shard_map/reduce_scatter | solution.py:83
  99.0 122.5 %reduce-scatter.3.cloned.1.call-start = ((), (), s32[]{:S(2)}) async-start(), calls=%async_computation.8 | async-start | bytes 1966080 | tf_op jit(solution)/shard_map/reduce_scatter | solution.py:101
  125.4 1.2 copy-start.2
  126.8 54.0 %copy-start.5 = (bf16[1152,128]{1,0:T(8,128)(2,1)S(1)}, bf16[1152,128]{1,0:T(8,128)(2,1)}, u32[]{:S(2)}) copy-start(bf16[1152,128]{1,0:T(8,128)(2,1)} %copy-done.4) | copy-start | bytes 884740
  176.1 10.9 %all-to-all-start.5 = ((bf16[8,24,768]{2,1,0:T(8,128)(2,1)}), bf16[8,24,768]{2,1,0:T(8,128)(2,1)S(1)}, u32[]{:S(2)}, u32[]{:S(2)}) async-start(bf16[8,24,768]{2,1,0:T(8,128)(2,1)} %bitcast.44), calls=%async_computation.7 | async-start | bytes 589824 | tf_op jit(solution)/shard_map/all_to_all | solution.py:86
Sparse Core Ops, SparseCore 0:
  23.3 51.1 all-gather.4
  76.3 42.6 all-gather.6
  121.6 54.4 reduce-scatter.4
  179.4 42.1 reduce-scatter.2
